TPU v7x, 32 devices: a whole 2x2x4 slice. The times are simulated.
32 devices in a mesh: dp: 2 (over x), row: 4 (over y, core), col: 4 (over z).
Axes of the slice: x: 2, y: 2, z: 4, core: 2. Of those that a mesh axis runs over, the one named last changes fastest.
Arguments:
- tokens: bfloat16 [768, 39200], P('row', ('dp', 'col')), may hold values from -6 to 6
- grad_out: bfloat16 [768, 39200], P('row', ('dp', 'col')), may hold values from -6 to 6
- adapter_index: int32 [8, 1], replicated, may hold values from 0 to 7
- norm1_gain: bfloat16 [768], P('row'), may hold values from 0.099609375 to 1.8984375
- norm2_gain: bfloat16 [768], P('row'), may hold values from 0.099609375 to 1.8984375
- qkv_weight: bfloat16 [768, 2304], P('row', 'col'), may hold values from -0.21875 to 0.21875
- proj_weight: bfloat16 [768, 768], P('col', 'row'), may hold values from -0.875 to 0.875
- fc1_weight: bfloat16 [768, 3072], P('row', 'col'), may hold values from -0.21875 to 0.21875
- fc2_weight: bfloat16 [768, 3072], P('row', 'col'), may hold values from -0.109375 to 0.109375
- rel_h: bfloat16 [27, 64], replicated, may hold values from -0.59765625 to 0.59765625
- rel_w: bfloat16 [27, 64], replicated, may hold values from -0.59765625 to 0.59765625
- qkv_down: bfloat16 [8, 768, 16], P(None, 'row'), may hold values from -0.21875 to 0.21875
- qkv_up: bfloat16 [8, 16, 2304], P(None, None, 'col'), may hold values from -0.75 to 0.75
- proj_down: bfloat16 [8, 768, 16], P(None, 'col'), may hold values from -0.21875 to 0.21875
- proj_up: bfloat16 [8, 16, 768], P(None, None, 'row'), may hold values from -0.75 to 0.75
- fc1_down: bfloat16 [8, 768, 16], P(None, 'row'), may hold values from -0.21875 to 0.21875
- fc1_up: bfloat16 [8, 16, 3072], P(None, None, 'col'), may hold values from -0.75 to 0.75
- fc2_down: bfloat16 [8, 3072, 16], P(None, 'col'), may hold values from -0.109375 to 0.109375
- fc2_up: bfloat16 [8, 16, 768], P(None, None, 'row'), may hold values from -0.75 to 0.75
Outputs:
- out: bfloat16 [768, 39200], P('row', ('dp', 'col'))
- tokens_grad: float32 [768, 39200], P('row', ('dp', 'col'))
- qkv_down_grad: float32 [8, 768, 16], P(None, 'row')
- qkv_up_grad: float32 [8, 16, 2304], P(None, None, 'col')
- proj_down_grad: float32 [8, 768, 16], P(None, 'col')
- proj_up_grad: float32 [8, 16, 768], P(None, None, 'row')
- fc1_down_grad: float32 [8, 768, 16], P(None, 'row')
- fc1_up_grad: float32 [8, 16, 3072], P(None, None, 'col')
- fc2_down_grad: float32 [8, 3072, 16], P(None, 'col')
- fc2_up_grad: float32 [8, 16, 768], P(None, None, 'row')
Inputs may be any that keep to these rules, and one draw needn't show every extreme that they name: `adapter_index`: every one of the 8 adapters is chosen by at least one image.
All inputs are finite; a program needn't handle non-finite values.
Results may differ from a plain program's by a relative error of at most 0.015.
Values may be sent and summed in bfloat16 or wider, within the bound.
No kernel may reach another device: no remote copies, remote signals or barrier semaphores. Data moves between devices by JAX's collectives and lax.ppermute only.
A program may use at most 448 MiB of HBM per device.

v0:
```python
import jax
import jax.numpy as jnp
from jax import lax
from jax.sharding import PartitionSpec as P

D = 768
HD = 64
WIN = 14
SIDE = 64
ADAPT = 8
NWIN_SIDE = 5
IMG_TOK = 4900
PRECISE = lax.Precision.HIGHEST
EPSILON = 1e-06


def exact_gelu(values):
    return jax.nn.gelu(values, approximate=False)


def valid_rows():
    position = jnp.arange(IMG_TOK, dtype=jnp.int32)
    window = position // (WIN * WIN)
    inside = position % (WIN * WIN)
    image_row = window // NWIN_SIDE * WIN + inside // WIN
    image_col = window % NWIN_SIDE * WIN + inside % WIN
    return ((image_row < SIDE) & (image_col < SIDE)).astype(jnp.float32)


def rel_table(rel_param):
    offsets = (
        jnp.arange(WIN, dtype=jnp.int32)[:, None]
        - jnp.arange(WIN, dtype=jnp.int32)[None, :]
        + WIN
        - 1
    )
    one_hot = (
        offsets[:, :, None] == jnp.arange(2 * WIN - 1, dtype=jnp.int32)[None, None, :]
    ).astype(jnp.bfloat16)
    return jnp.einsum("akn,nc->akc", one_hot, rel_param, preferred_element_type=jnp.float32).astype(
        jnp.bfloat16
    )


def pick_one(adapter, own_pick):
    return jnp.einsum("a,ade->de", own_pick, adapter.astype(jnp.float32), precision=PRECISE).astype(
        jnp.bfloat16
    )


def row_totals(first_sum, second_sum):
    return lax.psum((first_sum, second_sum), "row")


def norm_forward(values):
    totals = row_totals(jnp.sum(values, axis=1), jnp.sum(values * values, axis=1))
    center = totals[0] / D
    inv_std = lax.rsqrt(totals[1] / D - center * center + EPSILON)
    return ((values - center[:, None]) * inv_std[:, None], inv_std)


def norm_backward(grad_normed, normed, inv_std):
    totals = row_totals(jnp.sum(grad_normed, axis=1), jnp.sum(grad_normed * normed, axis=1))
    return inv_std[:, None] * (
        grad_normed - totals[0][:, None] / D - normed * totals[1][:, None] / D
    )


def local_norm(values):
    center = jnp.sum(values, axis=1) / D
    inv_std = lax.rsqrt(jnp.sum(values * values, axis=1) / D - center * center + EPSILON)
    return ((values - center[:, None]) * inv_std[:, None], inv_std)


def local_norm_back(grad_normed, normed, inv_std):
    first_mean = jnp.sum(grad_normed, axis=1) / D
    second_mean = jnp.sum(grad_normed * normed, axis=1) / D
    return inv_std[:, None] * (grad_normed - first_mean[:, None] - normed * second_mean[:, None])


def to_features(values):
    return lax.all_to_all(
        values.astype(jnp.bfloat16), "row", split_axis=0, concat_axis=1, tiled=True
    ).astype(values.dtype)


def to_tokens(values):
    return lax.all_to_all(
        values.astype(jnp.bfloat16), "row", split_axis=1, concat_axis=0, tiled=True
    ).astype(values.dtype)


def token_rows(values):
    return lax.all_to_all(values, "row", split_axis=0, concat_axis=1, tiled=True)


def head_cols(values):
    return lax.all_to_all(values, "row", split_axis=1, concat_axis=0, tiled=True)


def head_sums(values):
    return lax.all_to_all(
        values.astype(jnp.bfloat16), "row", split_axis=1, concat_axis=0, tiled=True
    ).astype(values.dtype)


def adapted_local(inputs, weight, down_mat, up_mat):
    product = jnp.dot(inputs, weight, preferred_element_type=jnp.float32)
    reduced = jnp.dot(inputs, down_mat, preferred_element_type=jnp.float32)
    return product + jnp.dot(reduced, up_mat.astype(jnp.float32), precision=PRECISE)


def adapted_back(grads, weight, down_mat, up_mat):
    contract = (((1,), (1,)), ((), ()))
    product = lax.dot_general(grads, weight, contract, preferred_element_type=jnp.float32)
    reduced = lax.dot_general(grads, up_mat, contract, preferred_element_type=jnp.float32)
    return product + lax.dot_general(
        reduced, down_mat.astype(jnp.float32), contract, precision=PRECISE
    )


def pair_grads(inputs_m, grads_m, down_m, up_m):
    reduced = jnp.dot(inputs_m, down_m, preferred_element_type=jnp.float32)
    back_red = lax.dot_general(
        grads_m, up_m, (((1,), (1,)), ((), ())), preferred_element_type=jnp.float32
    )
    grad_down = jnp.einsum("td,tr->dr", inputs_m, back_red, precision=PRECISE)
    grad_up = jnp.einsum("tr,to->ro", reduced, grads_m, precision=PRECISE)
    return (grad_down, grad_up)


def spread_pick(own_pick, grad_mat):
    return jnp.einsum("a,de->ade", own_pick, grad_mat)


def take_block(full, dim, index, length):
    return lax.dynamic_slice_in_dim(full, index * length, length, dim)


def split_qkv(qkv_low):
    heads_local = qkv_low.shape[1] // (3 * HD)
    arranged = qkv_low.reshape(NWIN_SIDE * NWIN_SIDE, WIN * WIN, heads_local, 3, HD)
    return (arranged[:, :, :, 0], arranged[:, :, :, 1], arranged[:, :, :, 2])


def score_matrix(query_b, key_b, tables):
    windows = query_b.shape[0]
    heads_local = query_b.shape[2]
    dot_scores = jnp.einsum(
        "nqhc,nkhc->nhqk", query_b, key_b, preferred_element_type=jnp.float32
    ) * HD ** (-0.5)
    spatial = query_b.reshape(windows, WIN, WIN, heads_local, HD)
    rel_rows = jnp.einsum(
        "nabhc,akc->nhabk", spatial, tables[0], preferred_element_type=jnp.float32
    )
    rel_cols = jnp.einsum(
        "nabhc,bkc->nhabk", spatial, tables[1], preferred_element_type=jnp.float32
    )
    shaped = dot_scores.reshape(windows, heads_local, WIN, WIN, WIN, WIN)
    shaped = shaped + rel_rows[:, :, :, :, :, None] + rel_cols[:, :, :, :, None, :]
    return shaped.reshape(windows, heads_local, WIN * WIN, WIN * WIN)


def attend(qkv_low, tables):
    query_b, key_b, value_b = split_qkv(qkv_low)
    scores = score_matrix(query_b, key_b, tables)
    maxima = jnp.max(scores, axis=3, keepdims=True)
    exponent = jnp.exp(scores - maxima)
    sum_exp = jnp.sum(exponent, axis=3, keepdims=True)
    attn_prob = (exponent / sum_exp).astype(jnp.bfloat16)
    attended = jnp.einsum("nhqk,nkhc->nqhc", attn_prob, value_b, preferred_element_type=jnp.float32)
    log_total = (maxima + jnp.log(sum_exp))[:, :, :, 0]
    return (attended.reshape(IMG_TOK, attended.shape[2] * HD).astype(jnp.bfloat16), log_total)


def attend_back(qkv_low, log_total, grad_attended, tables):
    query_b, key_b, value_b = split_qkv(qkv_low)
    windows = query_b.shape[0]
    heads_local = query_b.shape[2]
    scores = score_matrix(query_b, key_b, tables)
    attn_exact = jnp.exp(scores - log_total[:, :, :, None])
    prob_low = attn_exact.astype(jnp.bfloat16)
    grad_o = grad_attended.reshape(windows, WIN * WIN, heads_local, HD)
    grad_v = jnp.einsum("nhqk,nqhc->nkhc", prob_low, grad_o, preferred_element_type=jnp.float32)
    grad_p = jnp.einsum("nqhc,nkhc->nhqk", grad_o, value_b, preferred_element_type=jnp.float32)
    centre = jnp.sum(grad_p * attn_exact, axis=3, keepdims=True)
    grad_s = (attn_exact * (grad_p - centre)).astype(jnp.bfloat16)
    grad_q = jnp.einsum(
        "nhqk,nkhc->nqhc", grad_s, key_b, preferred_element_type=jnp.float32
    ) * HD ** (-0.5)
    grad_k = jnp.einsum(
        "nhqk,nqhc->nkhc", grad_s, query_b, preferred_element_type=jnp.float32
    ) * HD ** (-0.5)
    split_grad = grad_s.astype(jnp.float32).reshape(windows, heads_local, WIN, WIN, WIN, WIN)
    along_rows = jnp.sum(split_grad, axis=5)
    along_cols = jnp.sum(split_grad, axis=4)
    rel_grad = jnp.einsum(
        "nhabk,akc->nabhc", along_rows, tables[0].astype(jnp.float32), precision=PRECISE
    )
    rel_grad = rel_grad + jnp.einsum(
        "nhabk,bkc->nabhc", along_cols, tables[1].astype(jnp.float32), precision=PRECISE
    )
    grad_q = grad_q + rel_grad.reshape(windows, WIN * WIN, heads_local, HD)
    stacked = jnp.stack([grad_q, grad_k, grad_v], axis=3)
    return stacked.reshape(IMG_TOK, heads_local * 3 * HD).astype(jnp.bfloat16)


def body(
    tokens,
    grad_out,
    adapter_index,
    norm1_gain,
    norm2_gain,
    qkv_weight,
    proj_weight,
    fc1_weight,
    fc2_weight,
    rel_h,
    rel_w,
    qkv_down,
    qkv_up,
    proj_down,
    proj_up,
    fc1_down,
    fc1_up,
    fc2_down,
    fc2_up,
):
    members = lax.axis_size("col")
    row_index = lax.axis_index("row")
    col_index = lax.axis_index("col")
    group_ids = lax.dynamic_slice_in_dim(
        adapter_index[:, 0], lax.axis_index("dp") * members, members, 0
    )
    chosen = (group_ids[:, None] == jnp.arange(ADAPT, dtype=jnp.int32)[None, :]).astype(jnp.float32)
    own_pick = chosen[col_index]
    validity = valid_rows()[:, None]
    tables = (rel_table(rel_h), rel_table(rel_w))
    inputs = tokens.astype(jnp.float32).T
    normed_one, inv_one = norm_forward(inputs)
    gain_one = norm1_gain.astype(jnp.float32)
    hidden_one = (normed_one * gain_one * validity).astype(jnp.bfloat16)
    qkv_part, proj_part, qkv_dn_part, proj_up_part = (
        lax.all_gather(qkv_weight, "row", axis=0, tiled=True),
        lax.all_gather(proj_weight, "row", axis=1, tiled=True),
        lax.all_gather(qkv_down, "row", axis=1, tiled=True),
        lax.all_gather(proj_up, "row", axis=2, tiled=True),
    )
    qkv_full, proj_full, qkv_up_all, proj_dn_all = (
        lax.all_gather(qkv_part, "col", axis=1, tiled=True),
        lax.all_gather(proj_part, "col", axis=0, tiled=True),
        lax.all_gather(qkv_up, "col", axis=2, tiled=True),
        lax.all_gather(proj_down, "col", axis=1, tiled=True),
    )
    qkv_dn = pick_one(qkv_dn_part, own_pick)
    qkv_upm = pick_one(qkv_up_all, own_pick)
    proj_dn = pick_one(proj_dn_all, own_pick)
    proj_upm = pick_one(proj_up_part, own_pick)
    hidden_rows = token_rows(hidden_one)
    qkv_rows_out = adapted_local(hidden_rows, qkv_full, qkv_dn, qkv_upm).astype(jnp.bfloat16)
    qkv_low = head_cols(qkv_rows_out)
    attended, log_total = attend(qkv_low, tables)
    attended_rows = token_rows(attended)
    branch = head_sums(adapted_local(attended_rows, proj_full, proj_dn, proj_upm))
    middle = inputs + branch
    grad_final = grad_out.astype(jnp.float32).T * validity
    weight_up, weight_stored, down_one, up_two, gain_full = (
        lax.all_gather(fc1_weight, "row", axis=0, tiled=True),
        lax.all_gather(fc2_weight, "row", axis=0, tiled=True),
        lax.all_gather(fc1_down, "row", axis=1, tiled=True),
        lax.all_gather(fc2_up, "row", axis=2, tiled=True),
        lax.all_gather(norm2_gain, "row", axis=0, tiled=True),
    )
    weight_up, weight_stored, up_one, down_two = (
        lax.all_gather(weight_up, "col", axis=1, tiled=True),
        lax.all_gather(weight_stored, "col", axis=1, tiled=True),
        lax.all_gather(fc1_up, "col", axis=2, tiled=True),
        lax.all_gather(fc2_down, "col", axis=1, tiled=True),
    )
    weight_down = weight_stored.T
    down_fc1 = pick_one(down_one, own_pick)
    up_fc1 = pick_one(up_one, own_pick)
    down_fc2 = pick_one(down_two, own_pick)
    up_fc2 = pick_one(up_two, own_pick)
    local_mid = to_features(middle)
    normed_two, inv_two = local_norm(local_mid)
    gain_two = gain_full.astype(jnp.float32)
    hidden_two = (normed_two * gain_two).astype(jnp.bfloat16)
    pre_act = adapted_local(hidden_two, weight_up, down_fc1, up_fc1)
    activated = exact_gelu(pre_act).astype(jnp.bfloat16)
    mlp_out = to_tokens(adapted_local(activated, weight_down, down_fc2, up_fc2))
    grad_local = to_features(grad_final).astype(jnp.bfloat16)
    grad_activ = adapted_back(grad_local, weight_down, down_fc2, up_fc2)
    gelu_value, gelu_back = jax.vjp(exact_gelu, pre_act)
    grad_pre = gelu_back(grad_activ)[0].astype(jnp.bfloat16)
    grad_hidden_two = adapted_back(grad_pre, weight_up, down_fc1, up_fc1)
    grad_middle = grad_final + to_tokens(
        local_norm_back(grad_hidden_two * gain_two, normed_two, inv_two)
    )
    fc1_local = pair_grads(hidden_two, grad_pre, down_fc1, up_fc1)
    fc2_local = pair_grads(activated, grad_local, down_fc2, up_fc2)
    summed_all = lax.psum(
        (
            spread_pick(own_pick, fc1_local[0]),
            spread_pick(own_pick, fc1_local[1]),
            spread_pick(own_pick, fc2_local[0]),
            spread_pick(own_pick, fc2_local[1]),
        ),
        ("dp", "row", "col"),
    )
    fc1_down_grad = take_block(summed_all[0], 1, row_index, fc1_down.shape[1])
    fc1_up_grad = take_block(summed_all[1], 2, col_index, fc1_up.shape[2])
    fc2_down_grad = take_block(summed_all[2], 1, col_index, fc2_down.shape[1])
    fc2_up_grad = take_block(summed_all[3], 2, row_index, fc2_up.shape[2])
    result = ((middle + mlp_out) * validity).astype(jnp.bfloat16).T
    grad_branch = grad_middle.astype(jnp.bfloat16)
    grad_branch_rows = token_rows(grad_branch)
    grad_attended = head_cols(
        adapted_back(grad_branch_rows, proj_full, proj_dn, proj_upm).astype(jnp.bfloat16)
    )
    grad_qkv = attend_back(qkv_low, log_total, grad_attended, tables)
    grad_qkv_rows = token_rows(grad_qkv)
    grad_hidden_one = head_sums(adapted_back(grad_qkv_rows, qkv_full, qkv_dn, qkv_upm))
    qkv_pair = pair_grads(hidden_rows, grad_qkv_rows, qkv_dn, qkv_upm)
    proj_pair = pair_grads(attended_rows, grad_branch_rows, proj_dn, proj_upm)
    attn_sums = lax.psum(
        (
            spread_pick(own_pick, qkv_pair[0]),
            spread_pick(own_pick, qkv_pair[1]),
            spread_pick(own_pick, proj_pair[0]),
            spread_pick(own_pick, proj_pair[1]),
        ),
        ("dp", "row", "col"),
    )
    qkv_down_grad = take_block(attn_sums[0], 1, row_index, qkv_down.shape[1])
    qkv_up_grad = take_block(attn_sums[1], 2, col_index, qkv_up.shape[2])
    proj_down_grad = take_block(attn_sums[2], 1, col_index, proj_down.shape[1])
    proj_up_grad = take_block(attn_sums[3], 2, row_index, proj_up.shape[2])
    grad_inputs = (
        grad_middle + norm_backward(grad_hidden_one * validity * gain_one, normed_one, inv_one)
    ).T
    return (
        result,
        grad_inputs,
        qkv_down_grad,
        qkv_up_grad,
        proj_down_grad,
        proj_up_grad,
        fc1_down_grad,
        fc1_up_grad,
        fc2_down_grad,
        fc2_up_grad,
    )


def solution(mesh):
    return jax.shard_map(
        body,
        mesh=mesh,
        in_specs=(
            P("row", ("dp", "col")),
            P("row", ("dp", "col")),
            P(),
            P("row"),
            P("row"),
            P("row", "col"),
            P("col", "row"),
            P("row", "col"),
            P("row", "col"),
            P(),
            P(),
            P(None, "row", None),
            P(None, None, "col"),
            P(None, "col", None),
            P(None, None, "row"),
            P(None, "row", None),
            P(None, None, "col"),
            P(None, "col", None),
            P(None, None, "row"),
        ),
        out_specs=(
            P("row", ("dp", "col")),
            P("row", ("dp", "col")),
            P(None, "row", None),
            P(None, None, "col"),
            P(None, "col", None),
            P(None, None, "row"),
            P(None, "row", None),
            P(None, None, "col"),
            P(None, "col", None),
            P(None, None, "row"),
        ),
        check_vma=False,
    )
```

profile of v0, /device:TPU:0, one launch (start us, length us, event | category | flops | bytes accessed | tf_op | source)
XLA Modules:
  0.0 1826.9 jit_solution(15166732212104624496)
XLA Ops:
  7.3 11.5 all_gather.51
  20.9 11.5 all-reduce.3
  46.7 118.0 %all_gather.54 = bf16[8,16,2304]{1,0,2:T(8,128)(2,1)} all-gather(bf16[8,16,576]{1,0,2:T(8,128)(2,1)S(1)} %copy.225), channel_id=1, replica_groups=mesh['dp'=2,'row'=4,'col'=4] {'col'}, dimensions={2}, use_global_device_ids=true | all-gather | bytes 737280 | tf_op jit(solution)/shard_map/all_gather | solution.py:252
  171.6 12.9 all_gather.62
  184.5 30.9 %all_gather.57 = bf16[8,768,16]{2,0,1:T(8,128)(2,1)S(1)} all-gather(bf16[8,192,16]{2,0,1:T(8,128)(2,1)} %copy.243), channel_id=1, replica_groups=mesh['dp'=2,'row'=4,'col'=4] {'col'}, dimensions={1}, use_global_device_ids=true | all-gather | bytes 245760 | tf_op jit(solution)/shard_map/all_gather | solution.py:253
  215.4 12.6 all_gather.53
  247.6 8.9 copy.226
  263.0 74.5 %all_gather.55 = bf16[192,768]{0,1:T(8,128)(2,1)S(1)} all-gather(bf16[192,192]{0,1:T(8,128)(2,1)S(1)} %copy.241), channel_id=1, replica_groups=mesh['dp'=2,'row'=4,'col'=4] {'row'}, dimensions={1}, use_global_device_ids=true | all-gather | bytes 368640 | tf_op jit(solution)/shard_map/all_gather | solution.py:245
  338.7 13.0 all_gather.58
  362.3 9.7 copy.227
  372.0 26.8 %reshape.211 = bf16[25,196,3,3,64]{1,0,4,3,2:T(8,128)(2,1)} reshape(bf16[4,1225,576]{1,0,2:T(4,128)(2,1)} %copy.227) | data formatting | bytes 11289600 | tf_op jit(solution)/shard_map/reshape | solution.py:142
  427.1 21.4 %add.271 = f32[25,3,14,14,14,14]{0,5,4,3,2,1:T(8,128)} broadcast(f32[25,3,14,14,14]{0,4,3,2,1:T(8,128)S(1)} %copy.236), dimensions={0,1,2,3,5} | broadcast | bytes 12348000 | tf_op jit(solution)/shard_map/add | solution.py:160
  448.6 64.5 %add.272 = f32[25,3,196,196]{0,3,2,1:T(8,128)} reshape(f32[25,3,14,14,14,14]{0,5,4,3,2,1:T(8,128)} %add.271) | data formatting | bytes 23049600 | tf_op jit(solution)/shard_map/add | solution.py:160
  513.1 39.1 %copy.237 = f32[25,3,196,196]{2,3,1,0:T(8,128)} copy(f32[25,3,196,196]{0,3,2,1:T(8,128)} %add.272) | data formatting | bytes 23049600 | tf_op jit(solution)/shard_map/add | solution.py:160
  563.4 22.8 %add.268 = f32[25,3,14,14,14,14]{0,5,4,3,2,1:T(8,128)} broadcast(f32[25,3,14,14,14]{0,4,3,2,1:T(8,128)} %copy.233), dimensions={0,1,2,3,4} | broadcast | bytes 12348000 | tf_op jit(solution)/shard_map/add | solution.py:160
  586.3 64.5 %add.269 = f32[25,3,196,196]{0,3,2,1:T(8,128)} reshape(f32[25,3,14,14,14,14]{0,5,4,3,2,1:T(8,128)} %add.268) | data formatting | bytes 23049600 | tf_op jit(solution)/shard_map/add | solution.py:160
  650.8 39.1 %copy.234 = f32[25,3,196,196]{2,3,1,0:T(8,128)} copy(f32[25,3,196,196]{0,3,2,1:T(8,128)} %add.269) | data formatting | bytes 23049600 | tf_op jit(solution)/shard_map/add | solution.py:160
  689.9 24.5 %fusion.132 = (f32[25,3,196]{2,1,0:T(4,128)S(1)}, f32[25,3,196,196]{2,3,1,0:T(8,128)}) fusion(f32[25,3,196,196]{2,3,1,0:T(8,128)} %copy.237, f32[25,3,196,196]{2,3,1,0:T(8,128)} %copy.234, bf16[25,196,3,1,64]{1,0,4,3,2:T(8,128)(2,1)} %get-tuple-element.37, bf16[25,196,3,1,64]{1,0,4,3,2:T(8,128)(2,1)S(1)} %copy-done.9), kind=kOutput, calls=%fused_computation.234 | convolution fusion | flops 380303744 | bytes 38396400 | tf_op jit(solution)/shard_map/nqhc,nkhc->nhqk/dot_general | solution.py:149
  714.4 9.8 fusion.6
  724.2 10.1 convert_bitcast_fusion.6
  763.8 10.6 all-to-all-done.2
  779.3 33.6 %all_gather.67 = bf16[8,16,768]{1,0,2:T(8,128)(2,1)S(1)} all-gather(bf16[8,16,192]{1,0,2:T(8,128)(2,1)} %copy.250), channel_id=1, replica_groups=mesh['dp'=2,'row'=4,'col'=4] {'row'}, dimensions={2}, use_global_device_ids=true | all-gather | bytes 245760 | tf_op jit(solution)/shard_map/all_gather | solution.py:271
  814.5 19.3 %all_gather.66 = bf16[8,3072,16]{1,2,0:T(8,128)(2,1)S(1)} all-gather(bf16[8,768,16]{1,2,0:T(8,128)(2,1)} %param.36), channel_id=1, replica_groups=mesh['dp'=2,'row'=4,'col'=4] {'col'}, dimensions={1}, use_global_device_ids=true | all-gather | bytes 983040 | tf_op jit(solution)/shard_map/all_gather | solution.py:278
  858.0 9.8 copy.292
  868.1 30.2 %all_gather.63 = bf16[8,16,3072]{2,1,0:T(8,128)(2,1)S(1)} all-gather(bf16[8,16,768]{2,1,0:T(8,128)(2,1)S(1)} %copy-done.72), channel_id=1, replica_groups=mesh['dp'=2,'row'=4,'col'=4] {'col'}, dimensions={2}, use_global_device_ids=true | all-gather | bytes 983040 | tf_op jit(solution)/shard_map/all_gather | solution.py:277
  928.8 11.8 fusion.137
  940.6 12.5 all-to-all-done.4
  975.9 41.4 %multiply_convert_fusion.1 = (bf16[1225,3072]{1,0:T(8,128)(2,1)}, f32[1225,3072]{1,0:T(8,128)}, f32[1225,3072]{1,0:T(8,128)}) fusion(f32[1225,3072]{1,0:T(8,128)S(1)} %fusion.135, f32[1225,16]{0,1:T(8,128)S(1)} %fusion.149, bf16[1,16,3072]{2,0,1:T(2,128)(2,1)S(1)} %fusion.64), kind=kOutput, calls=%fused_computation.9 | convolution fusion | flops 970905600 | bytes 52861504 | tf_op jit(solution)/shard_map/dot_general | solution.py:110
  1017.3 23.1 %add_convert_fusion = bf16[1225,3072]{1,0:T(8,128)(2,1)} fusion(f32[1225,3072]{1,0:T(8,128)} %get-tuple-element.32, f32[1225,3072]{1,0:T(8,128)} %fusion.137, f32[1225,3072]{1,0:T(8,128)} %get-tuple-element.51, f32[1225,16]{0,1:T(8,128)S(1)} %fusion.116, bf16[1,3072,16]{1,2,0:T(8,128)(2,1)S(1)} %copy.292), kind=kOutput, calls=%fused_computation.8 | convolution fusion | flops 778982400 | bytes 52861504 | tf_op jit(solution)/shard_map/dot_general | solution.py:117
  1062.8 26.9 %all_to_all.186 = bf16[1225,4,192]{0,2,1:T(8,128)(2,1)S(1)} all-to-all(bf16[1225,4,192]{0,2,1:T(8,128)(2,1)S(1)} %bitcast.307), channel_id=1, replica_groups=mesh['dp'=2,'row'=4,'col'=4] {'row'}, dimensions={1} | all-to-all | bytes 3763200 | tf_op jit(solution)/shard_map/all_to_all | solution.py:88
  1114.9 23.5 %all-to-all-done.8 = bf16[4,1225,192]{1,2,0:T(8,128)(2,1)S(1)} async-done(((bf16[4,1225,192]{1,2,0:T(8,128)(2,1)}), bf16[4,1225,192]{1,2,0:T(8,128)(2,1)S(1)}, u32[]{:S(2)}, u32[]{:S(2)}) %all-to-all-start.8) | async-done | bytes 1881632 | tf_op jit(solution)/shard_map/all_to_all | solution.py:94
  1154.1 9.9 fusion.136
  1187.7 9.3 reshape.212
  1197.0 11.3 convert_bitcast_fusion.5
  1208.2 21.7 %multiply_reduce_fusion = (f32[25,3,196]{2,1,0:T(4,128)S(1)}, f32[25,3,196,196]{2,3,1,0:T(8,128)}) fusion(f32[25,3,196,196]{2,3,1,0:T(8,128)} %get-tuple-element.50, f32[25,3,196]{2,1,0:T(4,128)S(1)} %log_add_fusion, bf16[25,196,3,1,64]{1,0,4,3,2:T(8,128)(2,1)} %get-tuple-element.35, bf16[25,196,3,64]{1,0,3,2:T(8,128)(2,1)S(1)} %reshape.212), kind=kOutput, calls=%fused_computation.2 | convolution fusion | flops 377422528 | bytes 26930400 | tf_op jit(solution)/shard_map/nqhc,nkhc->nhqk/dot_general | solution.py:185
  1230.0 11.2 multiply_convert_fusion
  1249.0 30.3 %copy.261 = f32[25,3,196,196]{0,3,2,1:T(8,128)} copy(bf16[25,3,196,196]{2,3,1,0:T(8,128)(2,1)} %copy-done.2) | data formatting | bytes 17287200 | tf_op jit(solution)/shard_map/reshape | solution.py:194
  1279.4 64.6 %reshape.221 = f32[25,3,14,14,14,14]{0,5,4,3,2,1:T(8,128)} reshape(f32[25,3,196,196]{0,3,2,1:T(8,128)} %copy.261) | data formatting | bytes 23049600 | tf_op jit(solution)/shard_map/reshape | solution.py:194
  1344.0 94.7 %fusion.128 = (f32[25,3,14,14,14]{0,4,3,2,1:T(8,128)}, f32[25,3,14,14,14]{0,4,3,2,1:T(8,128)}) fusion(f32[25,3,14,14,14,14]{0,5,4,3,2,1:T(8,128)} %reshape.221), kind=kLoop, calls=%fused_computation.231 | loop fusion | flops 5350800 | bytes 13171200 | tf_op jit(solution)/shard_map/reduce_sum | solution.py:195
  1438.7 10.2 fusion.14
  1464.8 8.9 reshape.215
  1494.7 11.8 copy.269
  1506.5 24.2 %convert_element_type.249 = bf16[4,1225,576]{1,0,2:T(4,128)(2,1)} reshape(bf16[25,196,3,3,64]{1,0,4,3,2:T(8,128)(2,1)} %copy.269) | data formatting | bytes 11289600 | tf_op jit(solution)/shard_map/convert_element_type | solution.py:205
  1577.8 31.0 %all-to-all-done.10 = bf16[4,1225,576]{1,2,0:T(8,128)(2,1)} async-done(((bf16[4,1225,576]{1,2,0:T(8,128)(2,1)}), bf16[4,1225,576]{1,2,0:T(8,128)(2,1)}, u32[]{:S(2)}, u32[]{:S(2)}) %all-to-all-start.10) | async-done | bytes 5644832 | tf_op jit(solution)/shard_map/all_to_all | solution.py:94
  1643.2 17.6 all-to-all-done.11
  1678.7 10.9 all-reduce.2
  1689.7 9.7 fusion.37
  1699.4 106.6 %all-reduce.6.cloned.1.call-done = (f32[8,768,16]{1,2,0:T(8,128)}, f32[8,16,2304]{2,1,0:T(8,128)}, f32[8,768,16]{1,2,0:T(8,128)}, f32[8,16,768]{2,1,0:T(8,128)},...) async-done(((f32[8,768,16]{1,2,0:T(8,128)}, f32[8,16,2304]{2,1,0:T(8,128)}, f32[8,768,16]{1,2,0:T(8,128)}, ...) | async-done | bytes 6291472 | tf_op jit(solution)/shard_map/psum | solution.py:326
  (370 shorter events, 457.7 us)
Async XLA Ops:
  7.2 354.6 %copy-start = (bf16[27,64]{1,0:T(8,128)(2,1)S(1)}, bf16[27,64]{1,0:T(8,128)(2,1)}, u32[]{:S(2)}) copy-start(bf16[27,64]{1,0:T(8,128)(2,1)} %param.28) | copy-start | bytes 10372
  7.2 12.9 copy-start.90
  7.2 12.9 copy-start.4
  7.2 225.9 %all-gather.7.cloned.1.call-start = ((), (), s32[]{:S(2)}) async-start(), calls=%async_computation.12 | async-start | bytes 4423680 | tf_op jit(solution)/shard_map/all_gather | solution.py:250
  20.1 14.9 copy-start.86
  41.5 191.2 %all-to-all-start = ((bf16[4,1225,192]{1,2,0:T(8,128)(2,1)}), bf16[4,1225,192]{1,2,0:T(8,128)(2,1)S(1)}, u32[]{:S(2)}, u32[]{:S(2)}) async-start(bf16[4,1225,192]{1,2,0:T(8,128)(2,1)} %copy.222), calls=%async_computation | async-start | bytes 3932160 | tf_op jit(solution)/shard_map/all_to_all | solution.py:94
  45.1 119.6 %copy-start.76 = (bf16[8,192,16]{1,2,0:T(8,128)(2,1)S(1)}, bf16[8,192,16]{1,2,0:T(8,128)(2,1)}, u32[]{:S(2)}) copy-start(bf16[8,192,16]{1,2,0:T(8,128)(2,1)} %param.34) | copy-start | bytes 147460
  45.1 317.2 %all-gather.15.cloned.1.call-start = ((), (), s32[]{:S(2)}) async-start(), calls=%async_computation.16 | async-start | bytes 1474560 | tf_op jit(solution)/shard_map/all_gather | solution.py:269
  45.9 119.1 %copy-start.77 = (bf16[8,192,16]{1,2,0:T(8,128)(2,1)S(1)}, bf16[8,192,16]{1,2,0:T(8,128)(2,1)}, u32[]{:S(2)}) copy-start(bf16[8,192,16]{1,2,0:T(8,128)(2,1)} %param.32) | copy-start | bytes 147460
  45.9 120.1 %copy-start.78 = (bf16[8,192,16]{1,2,0:T(8,128)(2,1)S(1)}, bf16[8,192,16]{1,2,0:T(8,128)(2,1)}, u32[]{:S(2)}) copy-start(bf16[8,192,16]{1,2,0:T(8,128)(2,1)} %param.30) | copy-start | bytes 147460
  171.6 56.4 %copy-start.91 = (s32[8,1]{0,1:T(1,128)S(1)}, s32[8,1]{0,1:T(1,128)}, u32[]{:S(2)}) copy-start(s32[8,1]{0,1:T(1,128)} %param.21) | copy-start | bytes 100
  228.7 11.7 copy-start.51
  256.5 81.9 %copy-start.79 = (bf16[8,16,192]{2,1,0:T(8,128)(2,1)S(1)}, bf16[8,16,192]{2,1,0:T(8,128)(2,1)}, u32[]{:S(2)}) copy-start(bf16[8,16,192]{2,1,0:T(8,128)(2,1)} %param.33) | copy-start | bytes 147460
  256.5 105.8 %all-to-all-start.1 = ((bf16[1225,4,576]{0,2,1:T(8,128)(2,1)}), bf16[1225,4,576]{0,2,1:T(8,128)(2,1)}, u32[]{:S(2)}, u32[]{:S(2)}) async-start(bf16[1225,4,576]{0,2,1:T(8,128)(2,1)} %bitcast.293), calls=%async_computation.1 | async-start | bytes 11796480 | tf_op jit(solution)/shard_map/all_to_all | solution.py:98
  261.8 91.5 %copy-start.93 = (u32[32]{0:T(128)S(1)}, u32[32]{0:T(128)}, u32[]{:S(2)}) copy-start(u32[32]{0:T(128)} %constant.173) | copy-start | bytes 388
  261.8 92.7 %copy-start.92 = (bf16[192]{0:T(256)(128)(2,1)S(1)}, bf16[192]{0:T(256)(128)(2,1)}, u32[]{:S(2)}) copy-start(bf16[192]{0:T(256)(128)(2,1)} %param.23) | copy-start | bytes 1156
  261.8 100.2 %copy-start.89 = (bf16[27,64]{1,0:T(8,128)(2,1)S(1)}, bf16[27,64]{1,0:T(8,128)(2,1)}, u32[]{:S(2)}) copy-start(bf16[27,64]{1,0:T(8,128)(2,1)} %param.29) | copy-start | bytes 10372
  261.9 572.0 %all-gather.11.cloned.1.call-start = ((), (), s32[]{:S(2)}) async-start(), calls=%async_computation.14 | async-start | bytes 1474560 | tf_op jit(solution)/shard_map/all_gather | solution.py:268
  262.6 571.3 %all-gather.9.cloned.1.call-start = ((), (), s32[]{:S(2)}) async-start(), calls=%async_computation.13 | async-start | bytes 1474560 | tf_op jit(solution)/shard_map/all_gather | solution.py:251
  338.4 590.4 %all-gather.17.cloned.1.call-start = ((), (), s32[]{:S(2)}) async-start(), calls=%async_computation.17 | async-start | bytes 5898240 | tf_op jit(solution)/shard_map/all_gather | solution.py:276
  362.0 190.1 %copy-start.63 = (bf16[14,14,64,1,1]{2,1,4,3,0:T(8,128)(2,1)}, bf16[14,14,64,1,1]{2,1,4,3,0:T(8,128)(2,1)S(1)}, u32[]{:S(2)}) copy-start(bf16[14,14,64,1,1]{2,1,4,3,0:T(8,128)(2,1)S(1)} %fusion.61) | copy-start | bytes 75268
  362.2 55.7 %copy-start.65 = (bf16[14,14,64]{2,1,0:T(8,128)(2,1)}, bf16[14,14,64]{2,1,0:T(8,128)(2,1)S(1)}, u32[]{:S(2)}) copy-start(bf16[14,14,64]{2,1,0:T(8,128)(2,1)S(1)} %convolution_convert_fusion) | copy-start | bytes 75268
  405.0 13.0 copy-start.8
  650.8 39.1 %copy-start.9 = (bf16[25,196,3,1,64]{1,0,4,3,2:T(8,128)(2,1)S(1)}, bf16[25,196,3,1,64]{1,0,4,3,2:T(8,128)(2,1)}, u32[]{:S(2)}) copy-start(bf16[25,196,3,1,64]{1,0,4,3,2:T(8,128)(2,1)} %copy-done.8) | copy-start | bytes 5644804
  746.5 27.9 %all-to-all-start.2 = ((bf16[4,1225,192]{1,2,0:T(8,128)(2,1)}), bf16[4,1225,192]{1,2,0:T(8,128)(2,1)S(1)}, u32[]{:S(2)}, u32[]{:S(2)}) async-start(bf16[4,1225,192]{1,2,0:T(8,128)(2,1)} %copy.240), calls=%async_computation.2 | async-start | bytes 3932160 | tf_op jit(solution)/shard_map/all_to_all | solution.py:94
  775.7 70.0 %all-to-all-start.6 = ((bf16[4,1225,192]{1,2,0:T(8,128)(2,1)}), bf16[4,1225,192]{1,2,0:T(8,128)(2,1)S(1)}, u32[]{:S(2)}, u32[]{:S(2)}) async-start(bf16[4,1225,192]{1,2,0:T(8,128)(2,1)} %copy.253), calls=%async_computation.6 | async-start | bytes 3932160 | tf_op jit(solution)/shard_map/all_to_all | solution.py:82
  779.3 188.6 %all-gather.13.cloned.1.call-start = ((), (), s32[]{:S(2)}) async-start(), calls=%async_computation.15 | async-start | bytes 5898240 | tf_op jit(solution)/shard_map/all_gather | solution.py:275
  845.7 53.3 %copy-start.11 = (bf16[4,1225,192]{1,2,0:T(8,128)(2,1)}, bf16[4,1225,192]{1,2,0:T(8,128)(2,1)S(1)}, u32[]{:S(2)}) copy-start(bf16[4,1225,192]{1,2,0:T(8,128)(2,1)S(1)} %all-to-all-done.6) | copy-start | bytes 5644804
  845.7 53.6 %all-to-all-start.3 = ((bf16[1225,4,192]{0,2,1:T(8,128)(2,1)}), bf16[1225,4,192]{0,2,1:T(8,128)(2,1)}, u32[]{:S(2)}, u32[]{:S(2)}) async-start(bf16[1225,4,192]{0,2,1:T(8,128)(2,1)} %bitcast.305), calls=%async_computation.3 | async-start | bytes 3932160 | tf_op jit(solution)/shard_map/all_to_all | solution.py:102
  867.8 149.5 %copy-start.55 = (bf16[1,3072,16]{1,2,0:T(8,128)(2,1)}, bf16[1,3072,16]{1,2,0:T(8,128)(2,1)S(1)}, u32[]{:S(2)}) copy-start(bf16[1,3072,16]{1,2,0:T(8,128)(2,1)S(1)} %copy.292) | copy-start | bytes 294916
  868.1 30.9 %copy-start.69 = (bf16[1,16,768]{2,0,1:T(2,128)(2,1)}, bf16[1,16,768]{2,0,1:T(2,128)(2,1)S(1)}, u32[]{:S(2)}) copy-start(bf16[1,16,768]{2,0,1:T(2,128)(2,1)S(1)} %fusion.119) | copy-start | bytes 73732
  899.3 118.0 %copy-start.61 = (f32[1225,16]{0,1:T(8,128)}, f32[1225,16]{0,1:T(8,128)S(1)}, u32[]{:S(2)}) copy-start(f32[1225,16]{0,1:T(8,128)S(1)} %fusion.116) | copy-start | bytes 235204
  924.1 29.0 %all-to-all-start.4 = ((bf16[4,1225,192]{1,2,0:T(8,128)(2,1)}), bf16[4,1225,192]{1,2,0:T(8,128)(2,1)}, u32[]{:S(2)}, u32[]{:S(2)}) async-start(bf16[4,1225,192]{1,2,0:T(8,128)(2,1)} %copy.247), calls=%async_computation.4 | async-start | bytes 3932160 | tf_op jit(solution)/shard_map/all_to_all | solution.py:82
  1109.1 29.3 %copy-start.68 = (bf16[1,16,768]{2,0,1:T(2,128)(2,1)S(1)}, bf16[1,16,768]{2,0,1:T(2,128)(2,1)}, u32[]{:S(2)}) copy-start(bf16[1,16,768]{2,0,1:T(2,128)(2,1)} %fusion.123) | copy-start | bytes 73732
  1110.5 27.9 %all-to-all-start.8 = ((bf16[4,1225,192]{1,2,0:T(8,128)(2,1)}), bf16[4,1225,192]{1,2,0:T(8,128)(2,1)S(1)}, u32[]{:S(2)}, u32[]{:S(2)}) async-start(bf16[4,1225,192]{1,2,0:T(8,128)(2,1)} %copy.256), calls=%async_computation.8 | async-start | bytes 3932160 | tf_op jit(solution)/shard_map/all_to_all | solution.py:94
  1149.2 14.9 slice-start
  1149.2 29.3 %all-to-all-start.9 = ((bf16[1225,4,192]{0,2,1:T(8,128)(2,1)}), bf16[1225,4,192]{0,2,1:T(8,128)(2,1)}, u32[]{:S(2)}, u32[]{:S(2)}) async-start(bf16[1225,4,192]{0,2,1:T(8,128)(2,1)} %bitcast.306), calls=%async_computation.9 | async-start | bytes 3932160 | tf_op jit(solution)/shard_map/all_to_all | solution.py:98
  1178.5 358.2 %all-to-all-start.5 = ((bf16[1225,4,192]{0,2,1:T(8,128)(2,1)}), bf16[1225,4,192]{0,2,1:T(8,128)(2,1)}, u32[]{:S(2)}, u32[]{:S(2)}) async-start(bf16[1225,4,192]{0,2,1:T(8,128)(2,1)} %bitcast.38), calls=%async_computation.5 | async-start | bytes 3932160 | tf_op jit(solution)/shard_map/all_to_all | solution.py:88
  1230.0 14.2 copy-start.10
  1343.9 94.8 %copy-start.66 = (bf16[14,14,64]{2,1,0:T(8,128)(2,1)S(1)}, bf16[14,14,64]{2,1,0:T(8,128)(2,1)}, u32[]{:S(2)}) copy-start(bf16[14,14,64]{2,1,0:T(8,128)(2,1)} %copy-done.65) | copy-start | bytes 75268
  1438.7 10.3 copy-start.14
  1438.7 10.3 copy-start.64
  1536.7 17.4 slice-start.2
  1536.7 72.1 %all-to-all-start.10 = ((bf16[4,1225,576]{1,2,0:T(8,128)(2,1)}), bf16[4,1225,576]{1,2,0:T(8,128)(2,1)}, u32[]{:S(2)}, u32[]{:S(2)}) async-start(bf16[4,1225,576]{1,2,0:T(8,128)(2,1)} %copy.270), calls=%async_computation.10 | async-start | bytes 11796480 | tf_op jit(solution)/shard_map/all_to_all | solution.py:94
  1571.9 37.0 %copy-start.52 = (bf16[1,16,2304]{2,0,1:T(2,128)(2,1)S(1)}, bf16[1,16,2304]{2,0,1:T(2,128)(2,1)}, u32[]{:S(2)}) copy-start(bf16[1,16,2304]{2,0,1:T(2,128)(2,1)} %copy-done.51) | copy-start | bytes 221188
  1627.2 33.6 %all-to-all-start.11 = ((bf16[1225,4,192]{0,2,1:T(8,128)(2,1)}), bf16[1225,4,192]{0,2,1:T(8,128)(2,1)}, u32[]{:S(2)}, u32[]{:S(2)}) async-start(bf16[1225,4,192]{0,2,1:T(8,128)(2,1)} %bitcast.304), calls=%async_computation.11 | async-start | bytes 3932160 | tf_op jit(solution)/shard_map/all_to_all | solution.py:102
  1631.8 174.2 %all-reduce.6.cloned.1.call-start = ((), (), s32[]{:S(2)}) async-start(), calls=%async_computation.18 | async-start | bytes 12582912 | tf_op jit(solution)/shard_map/psum | solution.py:326
  1689.6 130.2 %copy-start.1 = (bf16[27,64]{1,0:T(8,128)(2,1)S(1)}, bf16[27,64]{1,0:T(8,128)(2,1)}, u32[]{:S(2)}) copy-start(bf16[27,64]{1,0:T(8,128)(2,1)} %param.28) | copy-start | bytes 10372
  (68 other events, 430.7 us)
Sparse Core Ops, SparseCore 0:
  20.2 108.6 all-gather.6
  130.5 16.0 all-gather.14
  264.3 24.6 all-gather.10
  338.5 29.8 all-gather.8
  369.8 88.5 all-gather.16
  834.0 100.3 all-gather.12
  1643.3 162.6 all-reduce.5
where the time goes:
time: 1840 us; the launch traced here: 1830 us
  local copies, waits for them, and re-layouts  647 us (35%)
  blocking collectives  412 us (22%)
  matrix products  314 us (17%)
  waiting for transfers between devices  211 us (11%)
  other arithmetic  177 us (10%)
  starting transfers between devices  49.4 us (3%)
    add x6, local copies, waits for them, and re-layouts, score_matrix(): shaped + rel_rows[:, :, :, :, :, None] + rel_cols[:, :, :, :, None, :]  251 us
    all_gather x1, blocking collectives, body(): lax.all_gather(qkv_up, 'col', axis=2, tiled=True)  118 us
    psum x1, waiting for transfers between devices, body(): lax.psum((spread_pick(own_pick, qkv_pair[0]), spread_pick(own_pick, qkv_p...  107 us
    reshape x2, local copies, waits for them, and re-layouts, attend_back(): grad_s.astype(jnp.float32).reshape(windows, heads_local, WIN, WIN, WIN, WIN)  94.9 us
    reduce_sum x1, other arithmetic, attend_back(): along_rows = jnp.sum(split_grad, axis=5)  94.7 us
    all_gather x1, blocking collectives, body(): lax.all_gather(proj_weight, 'row', axis=1, tiled=True)  74.5 us
    all_to_all x4, waiting for transfers between devices, token_rows(): lax.all_to_all(values, 'row', split_axis=0, concat_axis=1, tiled=True)  65.1 us
    dot_general x4, matrix products, adapted_local(): jnp.dot(reduced, up_mat.astype(jnp.float32), precision=PRECISE)  53.4 us
  transfers between devices with their start and end apart: 18, of which 7 were waited for; matrix products, arithmetic and copies ran while one was open for 52% of the time, Pallas kernels for 0%

commit v1 on v0

--- a/solution.py
+++ b/solution.py
@@ -12,6 +12,18 @@
 IMG_TOK = 4900
 PRECISE = lax.Precision.HIGHEST
 EPSILON = 1e-06
+
+
+def collect(shard, axis, dim):
+    ways, here = (lax.axis_size(axis), lax.axis_index(axis))
+    grown, reach = (shard, 1)
+    while reach < ways:
+        theirs = lax.ppermute(grown, axis, [(d, d ^ reach) for d in range(ways)])
+        mine_first = jnp.concatenate([grown, theirs], axis=dim)
+        theirs_first = jnp.concatenate([theirs, grown], axis=dim)
+        grown = jnp.where(here & reach == 0, mine_first, theirs_first)
+        reach = 2 * reach
+    return grown
 
 
 def exact_gelu(values):
@@ -249,7 +261,7 @@
     qkv_full, proj_full, qkv_up_all, proj_dn_all = (
         lax.all_gather(qkv_part, "col", axis=1, tiled=True),
         lax.all_gather(proj_part, "col", axis=0, tiled=True),
-        lax.all_gather(qkv_up, "col", axis=2, tiled=True),
+        collect(qkv_up, "col", 2),
         lax.all_gather(proj_down, "col", axis=1, tiled=True),
     )
     qkv_dn = pick_one(qkv_dn_part, own_pick)

time: 1840 us -> 1770 us (0.962)
  blocking collectives: 412 us -> 324 us
    all_gather x1 -> x0, blocking collectives: 118 us -> none  [body(): lax.all_gather(qkv_up, 'col', axis=2, tiled=True)]
  transfers between devices with their start and end apart: 18 -> 20, of which waited for: 7 -> 8; matrix products, arithmetic and copies ran while one was open for 52% -> 55% of each run, Pallas kernels for 0% -> 0%
where the time goes in v1:
time: 1770 us; the launch traced here: 1750 us
  local copies, waits for them, and re-layouts  644 us (36%)
  blocking collectives  324 us (18%)
  matrix products  315 us (18%)
  waiting for transfers between devices  218 us (12%)
  other arithmetic  180 us (10%)
  starting transfers between devices  52.8 us (3%)
    add x6, local copies, waits for them, and re-layouts, score_matrix(): shaped + rel_rows[:, :, :, :, :, None] + rel_cols[:, :, :, :, None, :]  251 us
    psum x1, waiting for transfers between devices, body(): lax.psum((spread_pick(own_pick, qkv_pair[0]), spread_pick(own_pick, qkv_p...  107 us
    reshape x2, local copies, waits for them, and re-layouts, attend_back(): grad_s.astype(jnp.float32).reshape(windows, heads_local, WIN, WIN, WIN, WIN)  95.1 us
    reduce_sum x1, other arithmetic, attend_back(): along_rows = jnp.sum(split_grad, axis=5)  94.8 us
    all_gather x1, blocking collectives, body(): lax.all_gather(proj_weight, 'row', axis=1, tiled=True)  74.7 us
    all_to_all x4, waiting for transfers between devices, token_rows(): lax.all_to_all(values, 'row', split_axis=0, concat_axis=1, tiled=True)  65.1 us
    dot_general x4, matrix products, adapted_local(): jnp.dot(reduced, up_mat.astype(jnp.float32), precision=PRECISE)  53.5 us
    all_gather x1, blocking collectives, body(): lax.all_gather(proj_down, 'col', axis=1, tiled=True)  38.3 us
  transfers between devices with their start and end apart: 20, of which 8 were waited for; matrix products, arithmetic and copies ran while one was open for 55% of the time, Pallas kernels for 0%

profile of v1, /device:TPU:0, one launch (start us, length us, event | category | flops | bytes accessed | tf_op | source)
XLA Modules:
  0.0 1750.4 jit_solution(10698132049476670270)
XLA Ops:
  7.3 11.5 all_gather.48
  20.9 11.5 all-reduce.3
  47.9 30.9 %all_gather.58 = bf16[8,768,16]{2,0,1:T(8,128)(2,1)S(1)} all-gather(bf16[8,192,16]{2,0,1:T(8,128)(2,1)} %copy.246), channel_id=1, replica_groups=mesh['dp'=2,'row'=4,'col'=4] {'row'}, dimensions={1}, use_global_device_ids=true | all-gather | bytes 245760 | tf_op jit(solution)/shard_map/all_gather | solution.py:282
  80.8 38.3 %all_gather.53 = bf16[8,768,16]{2,0,1:T(8,128)(2,1)} all-gather(bf16[8,192,16]{2,0,1:T(8,128)(2,1)} %copy.240), channel_id=1, replica_groups=mesh['dp'=2,'row'=4,'col'=4] {'col'}, dimensions={1}, use_global_device_ids=true | all-gather | bytes 245760 | tf_op jit(solution)/shard_map/all_gather | solution.py:265
  120.9 17.0 all_gather.50
  170.9 9.4 copy.223
  186.5 74.7 %all_gather.51 = bf16[192,768]{0,1:T(8,128)(2,1)S(1)} all-gather(bf16[192,192]{0,1:T(8,128)(2,1)S(1)} %copy.238), channel_id=1, replica_groups=mesh['dp'=2,'row'=4,'col'=4] {'row'}, dimensions={1}, use_global_device_ids=true | all-gather | bytes 368640 | tf_op jit(solution)/shard_map/all_gather | solution.py:257
  262.5 13.0 all_gather.54
  286.1 9.7 copy.224
  295.8 26.8 %reshape.211 = bf16[25,196,3,3,64]{1,0,4,3,2:T(8,128)(2,1)} reshape(bf16[4,1225,576]{1,0,2:T(4,128)(2,1)} %copy.224) | data formatting | bytes 11289600 | tf_op jit(solution)/shard_map/reshape | solution.py:154
  350.7 21.4 %add.271 = f32[25,3,14,14,14,14]{0,5,4,3,2,1:T(8,128)} broadcast(f32[25,3,14,14,14]{0,4,3,2,1:T(8,128)S(1)} %copy.233), dimensions={0,1,2,3,5} | broadcast | bytes 12348000 | tf_op jit(solution)/shard_map/add | solution.py:172
  372.1 64.5 %add.272 = f32[25,3,196,196]{0,3,2,1:T(8,128)} reshape(f32[25,3,14,14,14,14]{0,5,4,3,2,1:T(8,128)} %add.271) | data formatting | bytes 23049600 | tf_op jit(solution)/shard_map/add | solution.py:172
  436.6 39.1 %copy.234 = f32[25,3,196,196]{2,3,1,0:T(8,128)} copy(f32[25,3,196,196]{0,3,2,1:T(8,128)} %add.272) | data formatting | bytes 23049600 | tf_op jit(solution)/shard_map/add | solution.py:172
  487.0 22.8 %add.268 = f32[25,3,14,14,14,14]{0,5,4,3,2,1:T(8,128)} broadcast(f32[25,3,14,14,14]{0,4,3,2,1:T(8,128)} %copy.230), dimensions={0,1,2,3,4} | broadcast | bytes 12348000 | tf_op jit(solution)/shard_map/add | solution.py:172
  509.8 64.5 %add.269 = f32[25,3,196,196]{0,3,2,1:T(8,128)} reshape(f32[25,3,14,14,14,14]{0,5,4,3,2,1:T(8,128)} %add.268) | data formatting | bytes 23049600 | tf_op jit(solution)/shard_map/add | solution.py:172
  574.3 39.1 %copy.231 = f32[25,3,196,196]{2,3,1,0:T(8,128)} copy(f32[25,3,196,196]{0,3,2,1:T(8,128)} %add.269) | data formatting | bytes 23049600 | tf_op jit(solution)/shard_map/add | solution.py:172
  613.4 24.8 %fusion.133 = (f32[25,3,196]{2,1,0:T(4,128)S(1)}, f32[25,3,196,196]{2,3,1,0:T(8,128)}) fusion(f32[25,3,196,196]{2,3,1,0:T(8,128)} %copy.234, f32[25,3,196,196]{2,3,1,0:T(8,128)} %copy.231, bf16[25,196,3,1,64]{1,0,4,3,2:T(8,128)(2,1)} %get-tuple-element.37, bf16[25,196,3,1,64]{1,0,4,3,2:T(8,128)(2,1)S(1)} %copy-done.9), kind=kOutput, calls=%fused_computation.237 | convolution fusion | flops 380303744 | bytes 38396400 | tf_op jit(solution)/shard_map/nqhc,nkhc->nhqk/dot_general | solution.py:161
  638.2 9.8 fusion.6
  648.0 10.1 convert_bitcast_fusion.6
  687.3 10.6 all-to-all-done.2
  702.8 33.6 %all_gather.63 = bf16[8,16,768]{1,0,2:T(8,128)(2,1)S(1)} all-gather(bf16[8,16,192]{1,0,2:T(8,128)(2,1)} %copy.247), channel_id=1, replica_groups=mesh['dp'=2,'row'=4,'col'=4] {'row'}, dimensions={2}, use_global_device_ids=true | all-gather | bytes 245760 | tf_op jit(solution)/shard_map/all_gather | solution.py:283
  738.0 19.2 %all_gather.62 = bf16[8,3072,16]{1,2,0:T(8,128)(2,1)S(1)} all-gather(bf16[8,768,16]{1,2,0:T(8,128)(2,1)} %param.36), channel_id=1, replica_groups=mesh['dp'=2,'row'=4,'col'=4] {'col'}, dimensions={1}, use_global_device_ids=true | all-gather | bytes 983040 | tf_op jit(solution)/shard_map/all_gather | solution.py:290
  781.5 9.8 copy.289
  791.5 30.2 %all_gather.59 = bf16[8,16,3072]{2,1,0:T(8,128)(2,1)S(1)} all-gather(bf16[8,16,768]{2,1,0:T(8,128)(2,1)S(1)} %copy-done.71), channel_id=1, replica_groups=mesh['dp'=2,'row'=4,'col'=4] {'col'}, dimensions={2}, use_global_device_ids=true | all-gather | bytes 983040 | tf_op jit(solution)/shard_map/all_gather | solution.py:289
  852.4 11.9 fusion.138
  864.3 12.4 all-to-all-done.4
  899.5 41.5 %multiply_convert_fusion.1 = (bf16[1225,3072]{1,0:T(8,128)(2,1)}, f32[1225,3072]{1,0:T(8,128)}, f32[1225,3072]{1,0:T(8,128)}) fusion(f32[1225,3072]{1,0:T(8,128)S(1)} %fusion.136, f32[1225,16]{0,1:T(8,128)S(1)} %fusion.150, bf16[1,16,3072]{2,0,1:T(2,128)(2,1)S(1)} %fusion.64), kind=kOutput, calls=%fused_computation.9 | convolution fusion | flops 970905600 | bytes 52861504 | tf_op jit(solution)/shard_map/dot_general | solution.py:122
  941.0 22.8 %add_convert_fusion = bf16[1225,3072]{1,0:T(8,128)(2,1)} fusion(f32[1225,3072]{1,0:T(8,128)} %get-tuple-element.32, f32[1225,3072]{1,0:T(8,128)} %fusion.138, f32[1225,3072]{1,0:T(8,128)} %get-tuple-element.51, f32[1225,16]{0,1:T(8,128)S(1)} %fusion.118, bf16[1,3072,16]{1,2,0:T(8,128)(2,1)S(1)} %copy.289), kind=kOutput, calls=%fused_computation.8 | convolution fusion | flops 778982400 | bytes 52861504 | tf_op jit(solution)/shard_map/dot_general | solution.py:129
  969.2 8.7 fusion.139
  986.2 27.0 %all_to_all.186 = bf16[1225,4,192]{0,2,1:T(8,128)(2,1)S(1)} all-to-all(bf16[1225,4,192]{0,2,1:T(8,128)(2,1)S(1)} %bitcast.306), channel_id=1, replica_groups=mesh['dp'=2,'row'=4,'col'=4] {'row'}, dimensions={1} | all-to-all | bytes 3763200 | tf_op jit(solution)/shard_map/all_to_all | solution.py:100
  1038.4 23.5 %all-to-all-done.8 = bf16[4,1225,192]{1,2,0:T(8,128)(2,1)S(1)} async-done(((bf16[4,1225,192]{1,2,0:T(8,128)(2,1)}), bf16[4,1225,192]{1,2,0:T(8,128)(2,1)S(1)}, u32[]{:S(2)}, u32[]{:S(2)}) %all-to-all-start.8) | async-done | bytes 1881632 | tf_op jit(solution)/shard_map/all_to_all | solution.py:106
  1077.7 9.9 fusion.137
  1111.0 9.3 reshape.212
  1120.3 11.2 convert_bitcast_fusion.5
  1131.6 21.7 %multiply_reduce_fusion = (f32[25,3,196]{2,1,0:T(4,128)S(1)}, f32[25,3,196,196]{2,3,1,0:T(8,128)}) fusion(f32[25,3,196,196]{2,3,1,0:T(8,128)} %get-tuple-element.50, f32[25,3,196]{2,1,0:T(4,128)S(1)} %log_add_fusion, bf16[25,196,3,1,64]{1,0,4,3,2:T(8,128)(2,1)} %get-tuple-element.35, bf16[25,196,3,64]{1,0,3,2:T(8,128)(2,1)S(1)} %reshape.212), kind=kOutput, calls=%fused_computation.2 | convolution fusion | flops 377422528 | bytes 26930400 | tf_op jit(solution)/shard_map/nqhc,nkhc->nhqk/dot_general | solution.py:197
  1153.3 11.2 multiply_convert_fusion
  1172.4 30.4 %copy.258 = f32[25,3,196,196]{0,3,2,1:T(8,128)} copy(bf16[25,3,196,196]{2,3,1,0:T(8,128)(2,1)} %copy-done.2) | data formatting | bytes 17287200 | tf_op jit(solution)/shard_map/reshape | solution.py:206
  1202.8 64.7 %reshape.221 = f32[25,3,14,14,14,14]{0,5,4,3,2,1:T(8,128)} reshape(f32[25,3,196,196]{0,3,2,1:T(8,128)} %copy.258) | data formatting | bytes 23049600 | tf_op jit(solution)/shard_map/reshape | solution.py:206
  1267.6 94.8 %fusion.129 = (f32[25,3,14,14,14]{0,4,3,2,1:T(8,128)}, f32[25,3,14,14,14]{0,4,3,2,1:T(8,128)}) fusion(f32[25,3,14,14,14,14]{0,5,4,3,2,1:T(8,128)} %reshape.221), kind=kLoop, calls=%fused_computation.234 | loop fusion | flops 5350800 | bytes 13171200 | tf_op jit(solution)/shard_map/reduce_sum | solution.py:207
  1362.3 10.0 fusion.14
  1388.4 8.9 reshape.215
  1418.3 11.8 copy.266
  1430.2 24.2 %convert_element_type.249 = bf16[4,1225,576]{1,0,2:T(4,128)(2,1)} reshape(bf16[25,196,3,3,64]{1,0,4,3,2:T(8,128)(2,1)} %copy.266) | data formatting | bytes 11289600 | tf_op jit(solution)/shard_map/convert_element_type | solution.py:217
  1501.4 31.0 %all-to-all-done.10 = bf16[4,1225,576]{1,2,0:T(8,128)(2,1)} async-done(((bf16[4,1225,576]{1,2,0:T(8,128)(2,1)}), bf16[4,1225,576]{1,2,0:T(8,128)(2,1)}, u32[]{:S(2)}, u32[]{:S(2)}) %all-to-all-start.10) | async-done | bytes 5644832 | tf_op jit(solution)/shard_map/all_to_all | solution.py:106
  1566.6 17.6 %all-to-all-done.11 = bf16[1225,4,192]{0,2,1:T(8,128)(2,1)} async-done(((bf16[1225,4,192]{0,2,1:T(8,128)(2,1)}), bf16[1225,4,192]{0,2,1:T(8,128)(2,1)}, u32[]{:S(2)}, u32[]{:S(2)}) %all-to-all-start.11) | async-done | bytes 1881632 | tf_op jit(solution)/shard_map/all_to_all | solution.py:114
  1602.2 10.9 all-reduce.2
  1613.2 9.7 fusion.37
  1622.9 106.5 %all-reduce.6.cloned.1.call-done = (f32[8,768,16]{1,2,0:T(8,128)}, f32[8,16,2304]{2,1,0:T(8,128)}, f32[8,768,16]{1,2,0:T(8,128)}, f32[8,16,768]{2,1,0:T(8,128)},...) async-done(((f32[8,768,16]{1,2,0:T(8,128)}, f32[8,16,2304]{2,1,0:T(8,128)}, f32[8,768,16]{1,2,0:T(8,128)}, ...) | async-done | bytes 6291472 | tf_op jit(solution)/shard_map/psum | solution.py:338
  (365 shorter events, 459.9 us)
Async XLA Ops:
  7.2 278.4 %copy-start = (bf16[27,64]{1,0:T(8,128)(2,1)S(1)}, bf16[27,64]{1,0:T(8,128)(2,1)}, u32[]{:S(2)}) copy-start(bf16[27,64]{1,0:T(8,128)(2,1)} %param.28) | copy-start | bytes 10372
  7.2 12.9 copy-start.86
  7.2 12.9 copy-start.4
  7.2 149.5 %all-gather.7.cloned.1.call-start = ((), (), s32[]{:S(2)}) async-start(), calls=%async_computation.12 | async-start | bytes 4423680 | tf_op jit(solution)/shard_map/all_gather | solution.py:262
  20.1 14.9 copy-start.82
  41.5 37.4 %copy-start.87 = (s32[8,1]{0,1:T(1,128)S(1)}, s32[8,1]{0,1:T(1,128)}, u32[]{:S(2)}) copy-start(s32[8,1]{0,1:T(1,128)} %param.21) | copy-start | bytes 100
  41.5 113.7 %all-to-all-start = ((bf16[4,1225,192]{1,2,0:T(8,128)(2,1)}), bf16[4,1225,192]{1,2,0:T(8,128)(2,1)S(1)}, u32[]{:S(2)}, u32[]{:S(2)}) async-start(bf16[4,1225,192]{1,2,0:T(8,128)(2,1)} %copy.220), calls=%async_computation | async-start | bytes 3932160 | tf_op jit(solution)/shard_map/all_to_all | solution.py:106
  45.2 240.8 %all-gather.15.cloned.1.call-start = ((), (), s32[]{:S(2)}) async-start(), calls=%async_computation.16 | async-start | bytes 1474560 | tf_op jit(solution)/shard_map/all_gather | solution.py:281
  45.2 92.6 %collective-permute-start = (bf16[8,16,576]{2,1,0:T(8,128)(2,1)}, bf16[8,16,576]{2,1,0:T(8,128)(2,1)}, u32[]{:S(2)}, u32[]{:S(2)}) collective-permute-start(bf16[8,16,576]{2,1,0:T(8,128)(2,1)} %param.31), channel_id=1, source_target_pairs={{0,1},{1,0},{2,3},{3,2},{4,5},{5,4},{6,7},{7,6},{8,9},{9,8},{10,11... | collective-permute-start | bytes 442376 | tf_op jit(solution)/shard_map/ppermute | solution.py:21
  137.8 16.9 copy-start.78
  137.9 16.9 copy-start.80
  139.2 15.4 collective-permute-start.1
  180.3 81.9 %copy-start.75 = (bf16[8,16,192]{2,1,0:T(8,128)(2,1)S(1)}, bf16[8,16,192]{2,1,0:T(8,128)(2,1)}, u32[]{:S(2)}) copy-start(bf16[8,16,192]{2,1,0:T(8,128)(2,1)} %param.33) | copy-start | bytes 147460
  180.3 105.8 %all-to-all-start.1 = ((bf16[1225,4,576]{0,2,1:T(8,128)(2,1)}), bf16[1225,4,576]{0,2,1:T(8,128)(2,1)}, u32[]{:S(2)}, u32[]{:S(2)}) async-start(bf16[1225,4,576]{0,2,1:T(8,128)(2,1)} %bitcast.292), calls=%async_computation.1 | async-start | bytes 11796480 | tf_op jit(solution)/shard_map/all_to_all | solution.py:110
  185.6 91.5 %copy-start.89 = (u32[32]{0:T(128)S(1)}, u32[32]{0:T(128)}, u32[]{:S(2)}) copy-start(u32[32]{0:T(128)} %constant.176) | copy-start | bytes 388
  185.6 92.7 %copy-start.88 = (bf16[192]{0:T(256)(128)(2,1)S(1)}, bf16[192]{0:T(256)(128)(2,1)}, u32[]{:S(2)}) copy-start(bf16[192]{0:T(256)(128)(2,1)} %param.23) | copy-start | bytes 1156
  185.6 100.2 %copy-start.85 = (bf16[27,64]{1,0:T(8,128)(2,1)S(1)}, bf16[27,64]{1,0:T(8,128)(2,1)}, u32[]{:S(2)}) copy-start(bf16[27,64]{1,0:T(8,128)(2,1)} %param.29) | copy-start | bytes 10372
  185.6 571.6 %all-gather.11.cloned.1.call-start = ((), (), s32[]{:S(2)}) async-start(), calls=%async_computation.14 | async-start | bytes 1474560 | tf_op jit(solution)/shard_map/all_gather | solution.py:280
  186.4 570.9 %all-gather.9.cloned.1.call-start = ((), (), s32[]{:S(2)}) async-start(), calls=%async_computation.13 | async-start | bytes 1474560 | tf_op jit(solution)/shard_map/all_gather | solution.py:263
  262.1 590.2 %all-gather.17.cloned.1.call-start = ((), (), s32[]{:S(2)}) async-start(), calls=%async_computation.17 | async-start | bytes 5898240 | tf_op jit(solution)/shard_map/all_gather | solution.py:288
  285.8 189.9 %copy-start.62 = (bf16[14,14,64,1,1]{2,1,4,3,0:T(8,128)(2,1)}, bf16[14,14,64,1,1]{2,1,4,3,0:T(8,128)(2,1)S(1)}, u32[]{:S(2)}) copy-start(bf16[14,14,64,1,1]{2,1,4,3,0:T(8,128)(2,1)S(1)} %fusion.61) | copy-start | bytes 75268
  286.0 55.5 %copy-start.64 = (bf16[14,14,64]{2,1,0:T(8,128)(2,1)}, bf16[14,14,64]{2,1,0:T(8,128)(2,1)S(1)}, u32[]{:S(2)}) copy-start(bf16[14,14,64]{2,1,0:T(8,128)(2,1)S(1)} %convolution_convert_fusion) | copy-start | bytes 75268
  328.8 12.8 copy-start.8
  574.3 39.1 %copy-start.9 = (bf16[25,196,3,1,64]{1,0,4,3,2:T(8,128)(2,1)S(1)}, bf16[25,196,3,1,64]{1,0,4,3,2:T(8,128)(2,1)}, u32[]{:S(2)}) copy-start(bf16[25,196,3,1,64]{1,0,4,3,2:T(8,128)(2,1)} %copy-done.8) | copy-start | bytes 5644804
  648.0 10.2 copy-start.52
  670.0 27.9 %all-to-all-start.2 = ((bf16[4,1225,192]{1,2,0:T(8,128)(2,1)}), bf16[4,1225,192]{1,2,0:T(8,128)(2,1)S(1)}, u32[]{:S(2)}, u32[]{:S(2)}) async-start(bf16[4,1225,192]{1,2,0:T(8,128)(2,1)} %copy.237), calls=%async_computation.2 | async-start | bytes 3932160 | tf_op jit(solution)/shard_map/all_to_all | solution.py:106
  699.2 69.9 %all-to-all-start.6 = ((bf16[4,1225,192]{1,2,0:T(8,128)(2,1)}), bf16[4,1225,192]{1,2,0:T(8,128)(2,1)S(1)}, u32[]{:S(2)}, u32[]{:S(2)}) async-start(bf16[4,1225,192]{1,2,0:T(8,128)(2,1)} %copy.250), calls=%async_computation.6 | async-start | bytes 3932160 | tf_op jit(solution)/shard_map/all_to_all | solution.py:94
  702.8 188.7 %all-gather.13.cloned.1.call-start = ((), (), s32[]{:S(2)}) async-start(), calls=%async_computation.15 | async-start | bytes 5898240 | tf_op jit(solution)/shard_map/all_gather | solution.py:287
  769.1 53.3 %copy-start.11 = (bf16[4,1225,192]{1,2,0:T(8,128)(2,1)}, bf16[4,1225,192]{1,2,0:T(8,128)(2,1)S(1)}, u32[]{:S(2)}) copy-start(bf16[4,1225,192]{1,2,0:T(8,128)(2,1)S(1)} %all-to-all-done.6) | copy-start | bytes 5644804
  769.1 53.7 %all-to-all-start.3 = ((bf16[1225,4,192]{0,2,1:T(8,128)(2,1)}), bf16[1225,4,192]{0,2,1:T(8,128)(2,1)}, u32[]{:S(2)}, u32[]{:S(2)}) async-start(bf16[1225,4,192]{0,2,1:T(8,128)(2,1)} %bitcast.304), calls=%async_computation.3 | async-start | bytes 3932160 | tf_op jit(solution)/shard_map/all_to_all | solution.py:114
  791.3 149.7 %copy-start.54 = (bf16[1,3072,16]{1,2,0:T(8,128)(2,1)}, bf16[1,3072,16]{1,2,0:T(8,128)(2,1)S(1)}, u32[]{:S(2)}) copy-start(bf16[1,3072,16]{1,2,0:T(8,128)(2,1)S(1)} %copy.289) | copy-start | bytes 294916
  791.5 30.9 %copy-start.68 = (bf16[1,16,768]{2,0,1:T(2,128)(2,1)}, bf16[1,16,768]{2,0,1:T(2,128)(2,1)S(1)}, u32[]{:S(2)}) copy-start(bf16[1,16,768]{2,0,1:T(2,128)(2,1)S(1)} %fusion.121) | copy-start | bytes 73732
  822.7 118.3 %copy-start.60 = (f32[1225,16]{0,1:T(8,128)}, f32[1225,16]{0,1:T(8,128)S(1)}, u32[]{:S(2)}) copy-start(f32[1225,16]{0,1:T(8,128)S(1)} %fusion.118) | copy-start | bytes 235204
  847.5 29.2 %all-to-all-start.4 = ((bf16[4,1225,192]{1,2,0:T(8,128)(2,1)}), bf16[4,1225,192]{1,2,0:T(8,128)(2,1)}, u32[]{:S(2)}, u32[]{:S(2)}) async-start(bf16[4,1225,192]{1,2,0:T(8,128)(2,1)} %copy.244), calls=%async_computation.4 | async-start | bytes 3932160 | tf_op jit(solution)/shard_map/all_to_all | solution.py:94
  1032.5 29.3 %copy-start.67 = (bf16[1,16,768]{2,0,1:T(2,128)(2,1)S(1)}, bf16[1,16,768]{2,0,1:T(2,128)(2,1)}, u32[]{:S(2)}) copy-start(bf16[1,16,768]{2,0,1:T(2,128)(2,1)} %fusion.125) | copy-start | bytes 73732
  1033.9 27.9 %all-to-all-start.8 = ((bf16[4,1225,192]{1,2,0:T(8,128)(2,1)}), bf16[4,1225,192]{1,2,0:T(8,128)(2,1)S(1)}, u32[]{:S(2)}, u32[]{:S(2)}) async-start(bf16[4,1225,192]{1,2,0:T(8,128)(2,1)} %copy.253), calls=%async_computation.8 | async-start | bytes 3932160 | tf_op jit(solution)/shard_map/all_to_all | solution.py:106
  1072.6 15.0 slice-start
  1072.6 29.4 %all-to-all-start.9 = ((bf16[1225,4,192]{0,2,1:T(8,128)(2,1)}), bf16[1225,4,192]{0,2,1:T(8,128)(2,1)}, u32[]{:S(2)}, u32[]{:S(2)}) async-start(bf16[1225,4,192]{0,2,1:T(8,128)(2,1)} %bitcast.305), calls=%async_computation.9 | async-start | bytes 3932160 | tf_op jit(solution)/shard_map/all_to_all | solution.py:110
  1102.0 358.3 %all-to-all-start.5 = ((bf16[1225,4,192]{0,2,1:T(8,128)(2,1)}), bf16[1225,4,192]{0,2,1:T(8,128)(2,1)}, u32[]{:S(2)}, u32[]{:S(2)}) async-start(bf16[1225,4,192]{0,2,1:T(8,128)(2,1)} %bitcast.38), calls=%async_computation.5 | async-start | bytes 3932160 | tf_op jit(solution)/shard_map/all_to_all | solution.py:100
  1153.3 14.2 copy-start.10
  1267.6 94.8 %copy-start.65 = (bf16[14,14,64]{2,1,0:T(8,128)(2,1)S(1)}, bf16[14,14,64]{2,1,0:T(8,128)(2,1)}, u32[]{:S(2)}) copy-start(bf16[14,14,64]{2,1,0:T(8,128)(2,1)} %copy-done.64) | copy-start | bytes 75268
  1362.3 10.0 copy-start.63
  1460.3 17.3 slice-start.2
  1460.3 72.1 %all-to-all-start.10 = ((bf16[4,1225,576]{1,2,0:T(8,128)(2,1)}), bf16[4,1225,576]{1,2,0:T(8,128)(2,1)}, u32[]{:S(2)}, u32[]{:S(2)}) async-start(bf16[4,1225,576]{1,2,0:T(8,128)(2,1)} %copy.267), calls=%async_computation.10 | async-start | bytes 11796480 | tf_op jit(solution)/shard_map/all_to_all | solution.py:106
  1495.5 37.0 %copy-start.51 = (bf16[1,16,2304]{2,0,1:T(2,128)(2,1)S(1)}, bf16[1,16,2304]{2,0,1:T(2,128)(2,1)}, u32[]{:S(2)}) copy-start(bf16[1,16,2304]{2,0,1:T(2,128)(2,1)} %copy-done.50) | copy-start | bytes 221188
  1550.7 33.6 %all-to-all-start.11 = ((bf16[1225,4,192]{0,2,1:T(8,128)(2,1)}), bf16[1225,4,192]{0,2,1:T(8,128)(2,1)}, u32[]{:S(2)}, u32[]{:S(2)}) async-start(bf16[1225,4,192]{0,2,1:T(8,128)(2,1)} %bitcast.303), calls=%async_computation.11 | async-start | bytes 3932160 | tf_op jit(solution)/shard_map/all_to_all | solution.py:114
  1555.2 174.2 %all-reduce.6.cloned.1.call-start = ((), (), s32[]{:S(2)}) async-start(), calls=%async_computation.18 | async-start | bytes 12582912 | tf_op jit(solution)/shard_map/psum | solution.py:338
  1613.2 130.1 %copy-start.1 = (bf16[27,64]{1,0:T(8,128)(2,1)S(1)}, bf16[27,64]{1,0:T(8,128)(2,1)}, u32[]{:S(2)}) copy-start(bf16[27,64]{1,0:T(8,128)(2,1)} %param.28) | copy-start | bytes 10372
  (66 other events, 432.0 us)
Sparse Core Ops, SparseCore 0:
  20.2 78.6 all-gather.6
  100.4 20.6 all-gather.14
  188.0 24.5 all-gather.10
  262.3 29.7 all-gather.8
  293.5 88.5 all-gather.16
  757.4 100.3 all-gather.12
  1566.8 162.6 all-reduce.5
